TPU v7x, 256 devices: a whole 4x4x8 slice. The times are simulated.
256 devices in a mesh: net: 32 (over x, z), scen: 8 (over y, core).
Axes of the slice: x: 4, y: 4, z: 8, core: 2. Of those that a mesh axis runs over, the one named last changes fastest.
Arguments:
- arc_flows: float32 [256, 262144], P('scen', 'net'), may hold values from 0 to 1
- node_duals: float32 [256, 65536], P('scen', 'net'), may hold values from -6 to 6
- demand: float32 [256, 65536], P('scen', 'net'), may hold values from -6 to 6
- excess: float32 [256], P('scen'), may hold values from 0 to 0.5
- risk_duals: float32 [256], P('scen'), may hold values from 0.2 to 6
- threshold: float32 [1], replicated, may hold values from -2.5 to -1.5
- arc_costs: float32 [262144], P('net'), may hold values from 0.05 to 0.75
- local_blocks: bfloat16 [2048, 4, 128, 128], P('net'), may hold values from -0.125 to 0.125
- head_blocks: bfloat16 [2048, 128, 128], P('net'), may hold values from -0.125 to 0.125
- local_index: int32 [2048, 4], P('net'), may hold values from 0 to 15
- head_index: int32 [2048], P('net'), may hold values from 0 to 511, as said below
Outputs:
- flows_next: float32 [256, 262144], P('scen', 'net')
- duals_next: float32 [256, 65536], P('scen', 'net')
- excess_next: float32 [256], P('scen')
- risk_next: float32 [256], P('scen')
- threshold_next: float32 [1], replicated
Inputs may be any that keep to these rules, and one draw needn't show every extreme that they name: Among the arc blocks of one device, at most 4 have their head node block on any one device of net (head_index // 16 names the device), and in every device's arc blocks some device of net is named exactly 4 times.
All inputs are finite; a program needn't handle non-finite values.
Results may differ from a plain program's by a relative error of at most 0.0021.
Values may be sent and summed in bfloat16 or wider, within the bound.
A program may use at most 128 MiB of HBM per device.

v0:
```python
import jax
import jax.numpy as jnp
from jax import lax
from jax.sharding import PartitionSpec as P

ROUNDS = 3
primal_step = 0.5
dual_step = 0.5
risk_step = 1.0
tail_weight = 2.0


def per_device(
    arc_flows,
    node_duals,
    demand,
    excess,
    risk_duals,
    threshold,
    arc_costs,
    local_blocks,
    head_blocks,
    local_index,
    head_index,
):
    block_rows = local_blocks.shape[-1]
    scen_rows = arc_flows.shape[0]
    arc_blks = head_index.shape[0]
    node_blks = node_duals.shape[1] // block_rows
    touches = local_index.shape[1]
    net_size = lax.axis_size("net")
    scen_size = lax.axis_size("scen")
    slot_cap = max(2, (2 * arc_blks + net_size - 1) // net_size)
    slot_count = net_size * slot_cap
    arc_total = arc_flows.shape[1] * net_size
    scen_total = scen_rows * scen_size
    select_prec = lax.Precision.HIGH
    peer_dev = head_index // node_blks
    target = head_index % node_blks
    peer_hot = (peer_dev[:, None] == jnp.arange(net_size, dtype=jnp.int32)[None, :]).astype(
        jnp.int32
    )
    earlier = jnp.cumsum(peer_hot, axis=0) - peer_hot
    slot_rank = jnp.sum(earlier * peer_hot, axis=1)
    slot_ids = peer_dev * slot_cap + slot_rank
    slot_hot = slot_ids[:, None] == jnp.arange(slot_count, dtype=jnp.int32)[None, :]
    arc_ids = jnp.arange(arc_blks, dtype=jnp.int32)
    slot_arc = jnp.max(jnp.where(slot_hot, arc_ids[:, None], -1), axis=0)
    slot_filled = slot_arc >= 0
    slot_source = jnp.maximum(slot_arc, 0)
    wanted = jnp.max(jnp.where(slot_hot, target[:, None], -1), axis=0).reshape(net_size, slot_cap)
    asked = lax.all_to_all(wanted, "net", split_axis=0, concat_axis=0, tiled=True)
    asked_hot = asked.reshape(-1)[:, None] == jnp.arange(node_blks, dtype=jnp.int32)[None, :]
    local_hot = local_index[:, :, None] == jnp.arange(node_blks, dtype=jnp.int32)[None, None, :]
    asked_wide = asked_hot.astype(jnp.float32)
    local_wide = local_hot.astype(jnp.float32)
    local_half = local_hot.astype(jnp.bfloat16)
    flow_now = arc_flows
    dual_now = node_duals
    level = threshold
    excess_now = excess
    risk_now = risk_duals
    for iteration in range(ROUNDS):
        dual_panel = dual_now.astype(jnp.bfloat16)
        dual_grid = dual_panel.reshape(scen_rows, node_blks, block_rows)
        gathered = lax.all_gather(dual_panel, "net", axis=1, tiled=True)
        head_rows = jnp.take(gathered.reshape(scen_rows, -1, block_rows), head_index, axis=1)
        pull_summed = jnp.einsum(
            "sjn,jmn->sjm", head_rows, head_blocks, preferred_element_type=jnp.float32
        )
        for touched in range(touches):
            local_rows = jnp.einsum(
                "sbn,jb->sjn", dual_grid, local_half[:, touched], preferred_element_type=jnp.float32
            ).astype(jnp.bfloat16)
            pull_summed = pull_summed + jnp.einsum(
                "sjn,jmn->sjm",
                local_rows,
                local_blocks[:, touched],
                preferred_element_type=jnp.float32,
            )
        pulled = pull_summed.reshape(scen_rows, arc_blks * block_rows)
        risk_mine = risk_now
        mean_risk = lax.psum(jnp.sum(risk_now), "scen") / scen_total
        flows_new = jnp.maximum(
            flow_now - primal_step * (risk_mine[:, None] * arc_costs[None, :] - pulled), 0.0
        )
        level_new = level - primal_step * (1.0 - mean_risk)
        flows_bar = 2.0 * flows_new - flow_now
        level_bar = 2.0 * level_new - level
        partial_value = jnp.sum(arc_costs[None, :] * flows_bar, axis=1) / arc_total
        excess_new = jnp.maximum(excess_now - primal_step * (tail_weight - risk_now), 0.0)
        excess_bar = 2.0 * excess_new - excess_now
        losses = lax.psum(partial_value, "net")
        risk_now = jnp.maximum(risk_now + risk_step * (losses - excess_bar - level_bar), 0.0)
        excess_now = excess_new
        flow_grid = flows_bar.astype(jnp.bfloat16).reshape(scen_rows, arc_blks, block_rows)
        own_terms = jnp.einsum(
            "sjm,jmn->sjn", flow_grid, head_blocks, preferred_element_type=jnp.float32
        )
        term_pack = jnp.where(
            slot_filled[None, :, None], jnp.take(own_terms, slot_source, axis=1), 0.0
        )
        arrived = lax.all_to_all(
            term_pack.reshape(scen_rows, net_size, slot_cap, block_rows),
            "net",
            split_axis=1,
            concat_axis=1,
            tiled=True,
        )
        head_terms = arrived.reshape(scen_rows, slot_count, block_rows)
        summed = jnp.einsum("sqn,qb->sbn", head_terms, asked_wide, precision=select_prec)
        local_terms = jnp.einsum(
            "sjm,jkmn->sjkn", flow_grid, local_blocks, preferred_element_type=jnp.float32
        )
        summed = summed + jnp.einsum(
            "sjkn,jkb->sbn", local_terms, local_wide, precision=select_prec
        )
        dual_now = dual_now + dual_step * (
            demand - summed.reshape(scen_rows, node_blks * block_rows)
        )
        flow_now = flows_new
        level = level_new
    return (flow_now, dual_now, excess_now, risk_now, level)


def solution(mesh):
    placed = (
        P("scen", "net"),
        P("scen", "net"),
        P("scen", "net"),
        P("scen"),
        P("scen"),
        P(),
        P("net"),
        P("net", None, None, None),
        P("net", None, None),
        P("net", None),
        P("net"),
    )
    return jax.shard_map(
        per_device,
        mesh=mesh,
        in_specs=placed,
        out_specs=(P("scen", "net"), P("scen", "net"), P("scen"), P("scen"), P()),
        check_vma=False,
    )
```

profile of v0, /device:TPU:0, one launch (start us, length us, event | category | flops | bytes accessed | tf_op | source)
XLA Modules:
  0.0 597.3 jit_solution(4962526115088580452)
XLA Ops:
  10.9 9.6 %all-to-all-start = ((s32[32,1,4]{2,1,0:T(1,128)}), s32[32,1,4]{2,1,0:T(1,128)S(1)}, u32[]{:S(2)}, u32[]{:S(2)}) async-start(s32[32,1,4]{2,1,0:T(1,128)} %bitcast.20), calls=%async_computation | async-start | bytes 32768 | tf_op jit(solution)/shard_map/all_to_all | solution.py:52
  27.9 3.8 fusion.16
  31.7 3.9 fusion.22
  35.6 58.6 %all-gather.4.cloned.1.call-done = bf16[32,65536]{1,0:T(8,128)(2,1)} async-done(((bf16[32,2048]{1,0:T(8,128)(2,1)}), bf16[32,65536]{1,0:T(8,128)(2,1)}) %all-gather.4.cloned.1.call-update) | async-done | bytes 4194320 | tf_op jit(solution)/shard_map/all_gather | solution.py:66
  94.2 4.9 copy_bitcast_fusion.2
  99.1 3.6 gather_fusion
  116.7 5.4 all-to-all-start.1
  125.6 4.8 convolution_bitcast_fusion.2
  133.5 36.8 %all-to-all-done.1 = f32[32,32,4,128]{3,0,2,1:T(8,128)} async-done(((f32[32,32,4,128]{3,0,2,1:T(8,128)}), f32[32,32,4,128]{3,0,2,1:T(8,128)}, u32[]{:S(2)}, u32[]{:S(2)}) %all-to-all-start.1) | async-done | bytes 2097184 | tf_op jit(solution)/shard_map/all_to_all | solution.py:103
  175.8 13.0 %psum.43 = f32[]{:T(128)} all-reduce(f32[]{:T(128)} %reduce_sum.64), channel_id=1, replica_groups=mesh['net'=32,'scen'=8] {'scen'}, use_global_device_ids=true, to_apply=%region_3.5 | all-reduce | flops 1 | bytes 8 | tf_op jit(solution)/shard_map/psum | solution.py:83
  190.2 72.1 %psum.42 = f32[32]{0:T(128)S(1)} all-reduce(f32[32]{0:T(128)S(1)} %broadcast_multiply_fusion.2), channel_id=1, replica_groups=mesh['net'=32,'scen'=8] {'net'}, use_global_device_ids=true, to_apply=%region_1.3 | all-reduce | flops 32 | bytes 256 | tf_op jit(solution)/shard_map/psum | solution.py:93
  268.9 3.9 fusion.14
  272.8 3.8 fusion.20
  276.5 4.9 copy_bitcast_fusion.1
  281.4 3.6 gather_fusion.2
  292.7 3.2 gather_fusion.3
  299.0 4.8 all-to-all-start.2
  305.5 4.8 convolution_bitcast_fusion.1
  310.3 3.8 fusion.102
  314.1 26.1 %all-to-all-done.2 = f32[32,32,4,128]{3,0,2,1:T(8,128)} async-done(((f32[32,32,4,128]{3,0,2,1:T(8,128)}), f32[32,32,4,128]{3,0,2,1:T(8,128)}, u32[]{:S(2)}, u32[]{:S(2)}) %all-to-all-start.2) | async-done | bytes 2097184 | tf_op jit(solution)/shard_map/all_to_all | solution.py:103
  345.3 13.1 %psum.45 = f32[]{:T(128)} all-reduce(f32[]{:T(128)} %get-tuple-element.16), channel_id=1, replica_groups=mesh['net'=32,'scen'=8] {'scen'}, use_global_device_ids=true, to_apply=%region_11.14 | all-reduce | flops 1 | bytes 8 | tf_op jit(solution)/shard_map/psum | solution.py:83
  359.1 74.1 %psum.44 = f32[32]{0:T(128)S(1)} all-reduce(f32[32]{0:T(128)S(1)} %broadcast_multiply_fusion.1), channel_id=1, replica_groups=mesh['net'=32,'scen'=8] {'net'}, use_global_device_ids=true, to_apply=%region_9.12 | all-reduce | flops 32 | bytes 256 | tf_op jit(solution)/shard_map/psum | solution.py:93
  436.9 3.8 fusion.6
  440.7 3.9 fusion.12
  444.6 3.8 fusion.18
  448.4 4.9 copy_bitcast_fusion
  453.3 3.6 gather_fusion.4
  465.4 3.2 gather_fusion.5
  471.7 4.8 all-to-all-start.3
  476.4 13.9 %psum.47 = f32[]{:T(128)} all-reduce(f32[]{:T(128)} %get-tuple-element.11), channel_id=1, replica_groups=mesh['net'=32,'scen'=8] {'scen'}, use_global_device_ids=true, to_apply=%region_15.18 | all-reduce | flops 1 | bytes 8 | tf_op jit(solution)/shard_map/psum | solution.py:83
  492.4 83.1 %psum.46 = f32[32]{0:T(128)S(1)} all-reduce(f32[32]{0:T(128)S(1)} %broadcast_multiply_fusion), channel_id=1, replica_groups=mesh['net'=32,'scen'=8] {'net'}, use_global_device_ids=true, to_apply=%region_13.16 | all-reduce | flops 32 | bytes 256 | tf_op jit(solution)/shard_map/psum | solution.py:93
  576.1 4.8 convolution_bitcast_fusion
  (143 shorter events, 86.3 us)
Async XLA Ops:
  7.2 95.6 %copy-start = (bf16[64,128,128]{2,1,0:T(8,128)(2,1)S(1)}, bf16[64,128,128]{2,1,0:T(8,128)(2,1)}, u32[]{:S(2)}) copy-start(bf16[64,128,128]{2,1,0:T(8,128)(2,1)} %param.23) | copy-start | bytes 6291460
  7.2 87.1 %all-gather.4.cloned.1.call-start = ((), (), s32[]{:S(2)}) async-start(), calls=%async_computation.4 | async-start | bytes 4325376 | tf_op jit(solution)/shard_map/all_gather | solution.py:66
  10.9 105.9 %all-to-all-start = ((s32[32,1,4]{2,1,0:T(1,128)}), s32[32,1,4]{2,1,0:T(1,128)S(1)}, u32[]{:S(2)}, u32[]{:S(2)}) async-start(s32[32,1,4]{2,1,0:T(1,128)} %bitcast.20), calls=%async_computation | async-start | bytes 32768 | tf_op jit(solution)/shard_map/all_to_all | solution.py:52
  102.7 2.4 copy-start.9
  102.7 2.4 copy-start.11
  102.7 2.5 copy-start.22
  105.2 3.0 copy-start.3
  105.2 3.0 copy-start.25
  105.2 3.0 copy-start.27
  108.8 15.3 %copy-start.1 = (f32[32,8192]{1,0:T(8,128)}, f32[32,8192]{1,0:T(8,128)S(1)}, u32[]{:S(2)}) copy-start(f32[32,8192]{1,0:T(8,128)S(1)} %get-tuple-element.21) | copy-start | bytes 3145732
  116.7 53.5 %all-to-all-start.1 = ((f32[32,32,4,128]{3,0,2,1:T(8,128)}), f32[32,32,4,128]{3,0,2,1:T(8,128)}, u32[]{:S(2)}, u32[]{:S(2)}) async-start(f32[32,32,4,128]{3,0,2,1:T(8,128)} %bitcast.330), calls=%async_computation.1 | async-start | bytes 4194304 | tf_op jit(solution)/shard_map/all_to_all | solution.py:103
  122.2 154.4 %all-gather.6.cloned.1.call-start = ((), (), s32[]{:S(2)}) async-start(), calls=%async_computation.5 | async-start | bytes 4325376 | tf_op jit(solution)/shard_map/all_gather | solution.py:66
  125.5 4.9 copy-start.26
  173.2 1.2 copy-start.5
  173.2 1.2 copy-start.16
  173.2 89.1 %copy-start.28 = (f32[32]{0:T(128)S(1)}, f32[32]{0:T(128)}, u32[]{:S(2)}) copy-start(f32[32]{0:T(128)} %param.18) | copy-start | bytes 388
  285.0 2.4 copy-start.10
  285.0 2.4 copy-start.12
  285.0 2.4 copy-start.23
  287.5 3.0 copy-start.2
  299.0 41.3 %all-to-all-start.2 = ((f32[32,32,4,128]{3,0,2,1:T(8,128)}), f32[32,32,4,128]{3,0,2,1:T(8,128)}, u32[]{:S(2)}, u32[]{:S(2)}) async-start(f32[32,32,4,128]{3,0,2,1:T(8,128)} %bitcast.331), calls=%async_computation.2 | async-start | bytes 4194304 | tf_op jit(solution)/shard_map/all_to_all | solution.py:103
  303.8 144.6 %all-gather.8.cloned.1.call-start = ((), (), s32[]{:S(2)}) async-start(), calls=%async_computation.6 | async-start | bytes 4325376 | tf_op jit(solution)/shard_map/all_gather | solution.py:66
  340.3 3.0 copy-start.24
  343.2 1.2 copy-start.14
  343.3 1.2 copy-start.17
  456.9 2.4 copy-start.6
  456.9 2.4 copy-start.7
  456.9 2.5 copy-start.8
  456.9 2.5 copy-start.21
  471.7 112.4 %all-to-all-start.3 = ((f32[32,32,4,128]{3,0,2,1:T(8,128)}), f32[32,32,4,128]{3,0,2,1:T(8,128)}, u32[]{:S(2)}, u32[]{:S(2)}) async-start(f32[32,32,4,128]{3,0,2,1:T(8,128)} %bitcast.329), calls=%async_computation.3 | async-start | bytes 4194304 | tf_op jit(solution)/shard_map/all_to_all | solution.py:103
  587.0 1.0 copy-start.18
  587.0 1.1 copy-start.20
  (4 other events, 3.3 us)
Sparse Core Ops, SparseCore 0:
  11.2 83.0 all-gather.3
  175.4 78.8 all-gather.5
  345.4 77.5 all-gather.7
where the time goes:
time: 606 us; the launch traced here: 597 us
  blocking collectives  269 us (44%)
  waiting for transfers between devices  122 us (20%)
  matrix products  85.9 us (14%)
  local copies, waits for them, and re-layouts  50.6 us (8%)
  other arithmetic  25.8 us (4%)
  starting transfers between devices  25.4 us (4%)
  between operations  18.5 us (3%)
    psum x3, blocking collectives, per_device(): losses = lax.psum(partial_value, 'net')  229 us
    all_to_all x3, waiting for transfers between devices, per_device(): lax.all_to_all(term_pack.reshape(scen_rows, net_size, slot_cap, block_row...  62.9 us
    all_gather x3, waiting for transfers between devices, per_device(): gathered = lax.all_gather(dual_panel, 'net', axis=1, tiled=True)  58.6 us
    dot_general x12, matrix products, per_device(): jnp.einsum('sjn,jmn->sjm', local_rows, local_blocks[:, touched], preferre...  41.3 us
    psum x3, blocking collectives, per_device(): mean_risk = lax.psum(jnp.sum(risk_now), 'scen') / scen_total  40 us
    all_to_all x3, starting transfers between devices, per_device(): lax.all_to_all(term_pack.reshape(scen_rows, net_size, slot_cap, block_row...  15 us
    reshape x3, local copies, waits for them, and re-layouts, per_device(): gathered.reshape(scen_rows, -1, block_rows)  14.6 us
    dot_general x3, matrix products, per_device(): jnp.einsum('sjm,jkmn->sjkn', flow_grid, local_blocks, preferred_element_t...  14.5 us
  transfers between devices with their start and end apart: 7, of which 3 were waited for; matrix products, arithmetic and copies ran while one was open for 17% of the time, Pallas kernels for 0%

commit v1 on v0

--- a/solution.py
+++ b/solution.py
@@ -63,7 +63,9 @@
     for iteration in range(ROUNDS):
         dual_panel = dual_now.astype(jnp.bfloat16)
         dual_grid = dual_panel.reshape(scen_rows, node_blks, block_rows)
-        gathered = lax.all_gather(dual_panel, "net", axis=1, tiled=True)
+        gathered = jnp.concatenate(
+            lax.all_to_all(jnp.stack([dual_panel] * lax.axis_size("net")), "net", 0, 0), axis=1
+        )
         head_rows = jnp.take(gathered.reshape(scen_rows, -1, block_rows), head_index, axis=1)
         pull_summed = jnp.einsum(
             "sjn,jmn->sjm", head_rows, head_blocks, preferred_element_type=jnp.float32

time: 606 us -> 811 us (1.34)
  blocking collectives: 269 us -> 387 us
  local copies, waits for them, and re-layouts: 50.6 us -> 104 us
  waiting for transfers between devices: 122 us -> 148 us
  starting transfers between devices: 25.4 us -> 47.7 us
  between operations: 18.5 us -> 5.33 us
    psum x3, blocking collectives: 229 us -> 345 us  [per_device(): losses = lax.psum(partial_value, 'net')]
    all_to_all x0 -> x3, waiting for transfers between devices: none -> 82.9 us  [per_device(): lax.all_to_all(jnp.stack([dual_panel] * lax.axis_size('net')), 'net', 0, 0)]
    all_gather x3 -> x0, waiting for transfers between devices: 58.6 us -> none  [per_device(): gathered = lax.all_gather(dual_panel, 'net', axis=1, tiled=True)]
    another operation x0 -> x9, local copies, waits for them, and re-layouts: none -> 50.2 us  [the longest x6 42.7 us: per_device(): gathered.reshape(scen_rows, -1, block_rows)]
    all_to_all x0 -> x3, starting transfers between devices: none -> 22.8 us  [per_device(): lax.all_to_all(jnp.stack([dual_panel] * lax.axis_size('net')), 'net', 0, 0)]
  transfers between devices with their start and end apart: 7 -> 7, of which waited for: 3 -> 3; matrix products, arithmetic and copies ran while one was open for 17% -> 14% of each run, Pallas kernels for 0% -> 0%
where the time goes in v1:
time: 811 us; the launch traced here: 803 us
  blocking collectives  387 us (48%)
  waiting for transfers between devices  148 us (18%)
  local copies, waits for them, and re-layouts  104 us (13%)
  matrix products  86 us (11%)
  starting transfers between devices  47.7 us (6%)
  other arithmetic  24.4 us (3%)
    psum x3, blocking collectives, per_device(): losses = lax.psum(partial_value, 'net')  345 us
    all_to_all x3, waiting for transfers between devices, per_device(): lax.all_to_all(jnp.stack([dual_panel] * lax.axis_size('net')), 'net', 0, 0)  82.9 us
    all_to_all x3, waiting for transfers between devices, per_device(): lax.all_to_all(term_pack.reshape(scen_rows, net_size, slot_cap, block_row...  65.3 us
    another operation x6, local copies, waits for them, and re-layouts, per_device(): gathered.reshape(scen_rows, -1, block_rows)  42.7 us
    psum x3, blocking collectives, per_device(): mean_risk = lax.psum(jnp.sum(risk_now), 'scen') / scen_total  42.3 us
    dot_general x12, matrix products, per_device(): jnp.einsum('sjn,jmn->sjm', local_rows, local_blocks[:, touched], preferre...  41.4 us
    all_to_all x3, starting transfers between devices, per_device(): lax.all_to_all(jnp.stack([dual_panel] * lax.axis_size('net')), 'net', 0, 0)  22.8 us
    all_to_all x3, starting transfers between devices, per_device(): lax.all_to_all(term_pack.reshape(scen_rows, net_size, slot_cap, block_row...  19.8 us
  transfers between devices with their start and end apart: 7, of which 3 were waited for; matrix products, arithmetic and copies ran while one was open for 14% of the time, Pallas kernels for 0%

profile of v1, /device:TPU:0, one launch (start us, length us, event | category | flops | bytes accessed | tf_op | source)
XLA Modules:
  0.0 802.6 jit_solution(3090485199507391193)
XLA Ops:
  4.3 9.9 %all-to-all-start = ((bf16[32,32,2048]{2,1,0:T(8,128)(2,1)}), bf16[32,32,2048]{2,1,0:T(8,128)(2,1)}, u32[]{:S(2)}, u32[]{:S(2)}) async-start(bf16[32,32,2048]{2,1,0:T(8,128)(2,1)} %stack.6), calls=%async_computation | async-start | bytes 8388608 | tf_op jit(solution)/shard_map/all_to_all | solution.py:67
  20.5 3.8 fusion.16
  24.4 3.9 fusion.22
  28.3 82.9 %all-to-all-done = bf16[32,32,2048]{2,1,0:T(8,128)(2,1)} async-done(((bf16[32,32,2048]{2,1,0:T(8,128)(2,1)}), bf16[32,32,2048]{2,1,0:T(8,128)(2,1)}, u32[]{:S(2)}, u32[]{:S(2)}) %all-to-all-start) | async-done | bytes 4194336 | tf_op jit(solution)/shard_map/all_to_all | solution.py:67
  111.1 5.1 all-to-all-start.1
  116.3 6.5 copy.80
  122.7 7.4 reshape_reshape.9
  130.1 6.9 copy.81
  154.6 10.2 %all-to-all-start.2 = ((f32[32,32,4,128]{3,0,2,1:T(8,128)}), f32[32,32,4,128]{3,0,2,1:T(8,128)}, u32[]{:S(2)}, u32[]{:S(2)}) async-start(f32[32,32,4,128]{3,0,2,1:T(8,128)} %bitcast.318), calls=%async_computation.2 | async-start | bytes 4194304 | tf_op jit(solution)/shard_map/all_to_all | solution.py:105
  167.7 4.8 convolution_bitcast_fusion.2
  175.6 38.8 %all-to-all-done.2 = f32[32,32,4,128]{3,0,2,1:T(8,128)} async-done(((f32[32,32,4,128]{3,0,2,1:T(8,128)}), f32[32,32,4,128]{3,0,2,1:T(8,128)}, u32[]{:S(2)}, u32[]{:S(2)}) %all-to-all-start.2) | async-done | bytes 2097184 | tf_op jit(solution)/shard_map/all_to_all | solution.py:105
  221.2 6.2 all-to-all-start.3
  228.0 15.5 %psum.43 = f32[]{:T(128)} all-reduce(f32[]{:T(128)} %reduce_sum.64), channel_id=1, replica_groups=mesh['net'=32,'scen'=8] {'scen'}, use_global_device_ids=true, to_apply=%region_3.5 | all-reduce | flops 1 | bytes 8 | tf_op jit(solution)/shard_map/psum | solution.py:85
  244.8 138.9 %psum.42 = f32[32]{0:T(128)S(1)} all-reduce(f32[32]{0:T(128)S(1)} %broadcast_multiply_fusion.2), channel_id=1, replica_groups=mesh['net'=32,'scen'=8] {'net'}, use_global_device_ids=true, to_apply=%region_1.3 | all-reduce | flops 32 | bytes 256 | tf_op jit(solution)/shard_map/psum | solution.py:95
  393.2 3.9 fusion.8
  397.1 6.5 copy.96
  403.5 7.4 reshape_reshape.10
  410.9 6.9 copy.97
  436.1 4.8 all-to-all-start.4
  442.3 4.8 convolution_bitcast_fusion.1
  451.0 26.5 %all-to-all-done.4 = f32[32,32,4,128]{3,0,2,1:T(8,128)} async-done(((f32[32,32,4,128]{3,0,2,1:T(8,128)}), f32[32,32,4,128]{3,0,2,1:T(8,128)}, u32[]{:S(2)}, u32[]{:S(2)}) %all-to-all-start.4) | async-done | bytes 2097184 | tf_op jit(solution)/shard_map/all_to_all | solution.py:105
  484.4 6.7 all-to-all-start.5
  491.1 13.5 %psum.45 = f32[]{:T(128)} all-reduce(f32[]{:T(128)} %get-tuple-element.16), channel_id=1, replica_groups=mesh['net'=32,'scen'=8] {'scen'}, use_global_device_ids=true, to_apply=%region_11.14 | all-reduce | flops 1 | bytes 8 | tf_op jit(solution)/shard_map/psum | solution.py:85
  506.4 129.7 %psum.44 = f32[32]{0:T(128)} all-reduce(f32[32]{0:T(128)} %broadcast_multiply_fusion.1), channel_id=1, replica_groups=mesh['net'=32,'scen'=8] {'net'}, use_global_device_ids=true, to_apply=%region_9.12 | all-reduce | flops 32 | bytes 256 | tf_op jit(solution)/shard_map/psum | solution.py:95
  640.2 3.9 fusion.12
  651.7 6.5 copy.107
  658.2 7.4 reshape_reshape.11
  665.6 6.8 copy.108
  691.4 4.8 all-to-all-start.6
  696.2 13.3 %psum.47 = f32[]{:T(128)} all-reduce(f32[]{:T(128)} %get-tuple-element.11), channel_id=1, replica_groups=mesh['net'=32,'scen'=8] {'scen'}, use_global_device_ids=true, to_apply=%region_15.18 | all-reduce | flops 1 | bytes 8 | tf_op jit(solution)/shard_map/psum | solution.py:85
  711.7 76.0 %psum.46 = f32[32]{0:T(128)S(1)} all-reduce(f32[32]{0:T(128)S(1)} %broadcast_multiply_fusion), channel_id=1, replica_groups=mesh['net'=32,'scen'=8] {'net'}, use_global_device_ids=true, to_apply=%region_13.16 | all-reduce | flops 32 | bytes 256 | tf_op jit(solution)/shard_map/psum | solution.py:95
  788.2 4.8 convolution_bitcast_fusion
  (175 shorter events, 122.4 us)
Async XLA Ops:
  0.6 140.0 %copy-start = (bf16[64,128,128]{2,1,0:T(8,128)(2,1)S(1)}, bf16[64,128,128]{2,1,0:T(8,128)(2,1)}, u32[]{:S(2)}) copy-start(bf16[64,128,128]{2,1,0:T(8,128)(2,1)} %param.23) | copy-start | bytes 6291460
  4.3 9.9 %copy-start.5 = (f32[32,2048]{1,0:T(8,128)S(1)}, f32[32,2048]{1,0:T(8,128)}, u32[]{:S(2)}) copy-start(f32[32,2048]{1,0:T(8,128)} %param.16) | copy-start | bytes 786436
  4.3 10.0 %copy-start.41 = (s32[64]{0:T(128)S(1)}, s32[64]{0:T(128)}, u32[]{:S(2)}) copy-start(s32[64]{0:T(128)} %param.25) | copy-start | bytes 772
  4.3 11.2 %copy-start.27 = (s32[64,4]{0,1:T(4,128)S(1)}, s32[64,4]{0,1:T(4,128)}, u32[]{:S(2)}) copy-start(s32[64,4]{0,1:T(4,128)} %param.24) | copy-start | bytes 3076
  4.3 106.9 %all-to-all-start = ((bf16[32,32,2048]{2,1,0:T(8,128)(2,1)}), bf16[32,32,2048]{2,1,0:T(8,128)(2,1)}, u32[]{:S(2)}, u32[]{:S(2)}) async-start(bf16[32,32,2048]{2,1,0:T(8,128)(2,1)} %stack.6), calls=%async_computation | async-start | bytes 8388608 | tf_op jit(solution)/shard_map/all_to_all | solution.py:67
  15.4 402.3 %copy-start.29 = (s32[1024]{0:T(1024)}, s32[1024]{0:T(1024)S(1)}, u32[]{:S(2)}) copy-start(s32[1024]{0:T(1024)S(1)} %pad_clamp_fusion.1) | copy-start | bytes 12292
  15.5 414.2 %copy-start.28 = (s32[1024]{0:T(1024)}, s32[1024]{0:T(1024)S(1)}, u32[]{:S(2)}) copy-start(s32[1024]{0:T(1024)S(1)} %pad_clamp_fusion) | copy-start | bytes 12292
  15.5 405.9 %copy-start.37 = (pred[64]{0:T(512)(128)(4,1)}, pred[64]{0:T(512)(128)(4,1)S(1)}, u32[]{:S(2)}) copy-start(pred[64]{0:T(512)(128)(4,1)S(1)} %compare_and_fusion) | copy-start | bytes 196
  15.5 417.3 %copy-start.30 = (pred[128]{0:T(512)(128)(4,1)}, pred[128]{0:T(512)(128)(4,1)S(1)}, u32[]{:S(2)}) copy-start(pred[128]{0:T(512)(128)(4,1)S(1)} %get-tuple-element.22) | copy-start | bytes 388
  15.5 417.3 %copy-start.32 = (pred[128]{0:T(512)(128)(4,1)}, pred[128]{0:T(512)(128)(4,1)S(1)}, u32[]{:S(2)}) copy-start(pred[128]{0:T(512)(128)(4,1)S(1)} %get-tuple-element.23) | copy-start | bytes 388
  111.1 43.5 %all-to-all-start.1 = ((s32[32,1,4]{2,1,0:T(1,128)}), s32[32,1,4]{2,1,0:T(1,128)S(1)}, u32[]{:S(2)}, u32[]{:S(2)}) async-start(s32[32,1,4]{2,1,0:T(1,128)} %bitcast.21), calls=%async_computation.1 | async-start | bytes 32768 | tf_op jit(solution)/shard_map/all_to_all | solution.py:52
  143.1 3.0 copy-start.3
  143.1 3.0 copy-start.25
  143.1 3.0 copy-start.34
  146.7 19.5 %copy-start.1 = (f32[32,8192]{1,0:T(8,128)}, f32[32,8192]{1,0:T(8,128)S(1)}, u32[]{:S(2)}) copy-start(f32[32,8192]{1,0:T(8,128)S(1)} %get-tuple-element.21) | copy-start | bytes 3145732
  154.6 59.8 %all-to-all-start.2 = ((f32[32,32,4,128]{3,0,2,1:T(8,128)}), f32[32,32,4,128]{3,0,2,1:T(8,128)}, u32[]{:S(2)}, u32[]{:S(2)}) async-start(f32[32,32,4,128]{3,0,2,1:T(8,128)} %bitcast.318), calls=%async_computation.2 | async-start | bytes 4194304 | tf_op jit(solution)/shard_map/all_to_all | solution.py:105
  221.2 162.5 %copy-start.39 = (f32[32]{0:T(128)S(1)}, f32[32]{0:T(128)}, u32[]{:S(2)}) copy-start(f32[32]{0:T(128)} %param.18) | copy-start | bytes 388
  221.2 175.9 %all-to-all-start.3 = ((bf16[32,32,2048]{2,1,0:T(8,128)(2,1)}), bf16[32,32,2048]{2,1,0:T(8,128)(2,1)}, u32[]{:S(2)}, u32[]{:S(2)}) async-start(bf16[32,32,2048]{2,1,0:T(8,128)(2,1)} %stack.7), calls=%async_computation.3 | async-start | bytes 8388608 | tf_op jit(solution)/shard_map/all_to_all | solution.py:67
  384.3 42.5 %copy-start.35 = (f32[32]{0:T(128)}, f32[32]{0:T(128)S(1)}, u32[]{:S(2)}) copy-start(f32[32]{0:T(128)S(1)} %get-tuple-element.17) | copy-start | bytes 388
  423.8 3.0 copy-start.2
  436.1 41.4 %all-to-all-start.4 = ((f32[32,32,4,128]{3,0,2,1:T(8,128)}), f32[32,32,4,128]{3,0,2,1:T(8,128)}, u32[]{:S(2)}, u32[]{:S(2)}) async-start(f32[32,32,4,128]{3,0,2,1:T(8,128)} %bitcast.319), calls=%async_computation.4 | async-start | bytes 4194304 | tf_op jit(solution)/shard_map/all_to_all | solution.py:105
  477.5 3.0 copy-start.24
  484.4 167.3 %all-to-all-start.5 = ((bf16[32,32,2048]{2,1,0:T(8,128)(2,1)}), bf16[32,32,2048]{2,1,0:T(8,128)(2,1)}, u32[]{:S(2)}, u32[]{:S(2)}) async-start(bf16[32,32,2048]{2,1,0:T(8,128)(2,1)} %stack.8), calls=%async_computation.5 | async-start | bytes 8388608 | tf_op jit(solution)/shard_map/all_to_all | solution.py:67
  665.6 10.6 %copy-start.38 = (pred[64]{0:T(512)(128)(4,1)S(1)}, pred[64]{0:T(512)(128)(4,1)}, u32[]{:S(2)}) copy-start(pred[64]{0:T(512)(128)(4,1)} %copy-done.37) | copy-start | bytes 196
  676.1 2.5 copy-start.10
  676.1 2.5 copy-start.22
  678.6 2.9 copy-start.26
  678.6 2.9 copy-start.36
  684.8 3.4 copy-start.31
  684.8 3.4 copy-start.33
  691.4 104.7 %all-to-all-start.6 = ((f32[32,32,4,128]{3,0,2,1:T(8,128)}), f32[32,32,4,128]{3,0,2,1:T(8,128)}, u32[]{:S(2)}, u32[]{:S(2)}) async-start(f32[32,32,4,128]{3,0,2,1:T(8,128)} %bitcast.317), calls=%async_computation.6 | async-start | bytes 4194304 | tf_op jit(solution)/shard_map/all_to_all | solution.py:105
  696.2 91.5 %copy-start.40 = (f32[32]{0:T(128)S(1)}, f32[32]{0:T(128)}, u32[]{:S(2)}) copy-start(f32[32]{0:T(128)} %get-tuple-element.13) | copy-start | bytes 388
  (17 other events, 28.6 us)
